TPU v7x, 256 devices: a whole 4x4x8 slice. The times are simulated.
256 devices in a mesh: lon: 64 (over z, x, y_hi), probe: 4 (over y_lo, core).
Axes of the slice: x: 4, y: 4 (y_hi: 2, y_lo: 2; y = y_hi * 2 + y_lo), z: 8, core: 2. Of those that a mesh axis runs over, the one named last changes fastest.
Arguments:
- increments: float32 [64, 1536, 8, 256], P('probe', 'lon'), may hold values from -6 to 6
- winds: float32 [2, 1536, 8, 256], P(None, 'lon'), may hold values from -0.2 to 0.2
- obs_weight: float32 [1536, 8, 256], P('lon'), may hold values from 0.1 to 10
Outputs:
- basis: float32 [64, 384, 512], P('probe', 'lon')
- upper: float32 [64, 64], replicated
All inputs are finite; a program needn't handle non-finite values.
Results may differ from a plain program's by a relative error of at most 0.00011.
Values sent between devices are 32-bit elements; how exact they have to be, the bound alone decides.
A program may use at most 128 MiB of HBM per device.

v0:
```python
import jax
import jax.numpy as jnp
from jax import lax
from jax.sharding import PartitionSpec as P


def from_behind(block, axis, distance):
    devices = range(lax.axis_size(axis))
    route = [((i - distance) % len(devices), i) for i in devices]
    return lax.ppermute(block, axis, route)


def butterfly_sum(block, axis):
    count = lax.axis_size(axis)
    if count & count - 1:
        return lax.psum(block, axis)
    distance = 1
    while distance < count:
        route = [(i, i ^ distance) for i in range(count)]
        block = block + lax.ppermute(block, axis, route)
        distance *= 2
    return block


def padded(block, sides, width):
    for axis, dim in sides:
        count = lax.axis_size(axis)
        forward = [(i, i + 1) for i in range(count - 1)]
        forward.append((count - 1, 0))
        backward = [(target, source) for source, target in forward]
        low = lax.ppermute(
            lax.slice_in_dim(block, block.shape[dim] - width, None, axis=dim), axis, forward
        )
        high = lax.ppermute(lax.slice_in_dim(block, 0, width, axis=dim), axis, backward)
        block = jnp.concatenate([low, block, high], axis=dim)
    return block


def lat_mask(field):
    rows = lax.broadcasted_iota(jnp.int32, field.shape, field.ndim - 1)
    return jnp.where(rows > 0, field, jnp.zeros_like(field))


def below(field):
    return jnp.concatenate([jnp.zeros_like(field[..., :1]), field[..., :-1]], axis=-1)


def above(field):
    return jnp.concatenate([field[..., 1:], jnp.zeros_like(field[..., :1])], axis=-1)


def forward_core(widened, east, north):
    a_pos = jnp.maximum(east, 0.0)
    b_neg = jnp.minimum(east, 0.0)
    c_pos = jnp.maximum(north[1:-1], 0.0)
    d_neg = jnp.minimum(north[1:-1], 0.0)
    flux_w = a_pos[1:] * widened[:, :-1] + b_neg[1:] * widened[:, 1:]
    inner = widened[:, 1:-1]
    flux_s = c_pos * below(inner) + d_neg * inner
    flux_n = above(flux_s)
    return inner - (flux_w[:, 1:] - flux_w[:, :-1]) - (flux_n - flux_s)


def adjoint_core(widened, east, north):
    a_pos = jnp.maximum(east, 0.0)
    b_neg = jnp.minimum(east, 0.0)[1:-1]
    c_pos = jnp.maximum(north[1:-1], 0.0)
    d_neg = jnp.minimum(north[1:-1], 0.0)
    a_east = a_pos[2:]
    c_north = above(c_pos)
    inner = widened[:, 1:-1]
    west_val = widened[:, :-2]
    east_val = widened[:, 2:]
    return (
        inner * (1.0 - a_east + b_neg - c_north + d_neg)
        - b_neg * west_val
        + a_east * east_val
        - d_neg * below(inner)
        + c_north * above(inner)
    )


def body(increments, winds, obs_weight):
    east_local = winds[0]
    north_local = lat_mask(winds[1])
    next_first = from_behind(east_local[:1], "lon", -1)
    near_east = jnp.concatenate([jnp.zeros_like(next_first), east_local, next_first], axis=0)
    edge_zero = jnp.zeros_like(north_local[:1])
    near_north = jnp.concatenate([edge_zero, north_local, edge_zero], axis=0)

    def widen(field):
        return padded(field, (("lon", 1),), 1)

    state = increments
    for step in range(2):
        state = forward_core(widen(state), near_east, near_north)
    state = obs_weight * state
    for step in range(2):
        state = adjoint_core(widen(state), near_east, near_north)
    sketch = increments + state
    probe_count, lon_count, level_count, lat_count = sketch.shape
    coarse = jnp.mean(
        sketch.reshape(probe_count, lon_count // 4, 4, level_count, lat_count // 4, 4), axis=(2, 5)
    )
    coarse = coarse.reshape(probe_count, -1)
    all_probes = probe_count * lax.axis_size("probe")
    ident = jnp.eye(all_probes, dtype=jnp.float32)
    full_panel = lax.all_gather(coarse, "probe", axis=0, tiled=True)
    local_gram = jnp.dot(
        full_panel,
        full_panel.T,
        precision=lax.Precision.HIGHEST,
        preferred_element_type=jnp.float32,
    )
    gram = butterfly_sum(local_gram, "lon")
    lower = jnp.linalg.cholesky(gram)
    inverse = lax.linalg.triangular_solve(lower, ident, left_side=True, lower=True)
    own_rows = lax.dynamic_slice_in_dim(
        inverse, lax.axis_index("probe") * probe_count, probe_count, 0
    )
    basis = jnp.dot(
        own_rows, full_panel, precision=lax.Precision.HIGHEST, preferred_element_type=jnp.float32
    )
    return (basis.reshape(probe_count, lon_count // 4, -1), lower.T)


def solution(mesh):
    in_specs = (P("probe", "lon", None, None), P(None, "lon", None, None), P("lon", None, None))
    out_specs = (P("probe", "lon", None), P())
    return jax.shard_map(body, mesh=mesh, in_specs=in_specs, out_specs=out_specs, check_vma=False)
```

profile of v0, /device:TPU:8, one launch (start us, length us, event | category | flops | bytes accessed | tf_op | source)
XLA Modules:
  0.0 148.9 jit_solution(1681838737861612050)
XLA Ops:
  1.3 9.8 %collective-permute-start = (f32[1,8,256]{2,1,0:T(8,128)S(1)}, f32[1,8,256]{2,1,0:T(8,128)S(1)}, u32[]{:S(2)}, u32[]{:S(2)}) collective-permute-start(f32[1,8,256]{2,1,0:T(8,128)S(1)} %slice_bitcast_fusion.1), channel_id=1, source_target_pairs={{4,0},{8,4},{12,8},{16,12},{20,16},{24,20},{28,24},{32,28},{36,32}... | collective-permute-start | bytes 24584 | tf_op jit(solution)/shard_map/ppermute | solution.py:10
  11.1 1.0 fusion.34
  12.2 7.7 %collective-permute-start.2 = (f32[16,1,8,256]{3,2,1,0:T(8,128)S(1)}, f32[16,1,8,256]{3,2,1,0:T(8,128)S(1)}, u32[]{:S(2)}, u32[]{:S(2)}) collective-permute-start(f32[16,1,8,256]{3,2,1,0:T(8,128)S(1)} %get-tuple-element.22), channel_id=1, source_target_pairs={{4,0},{8,4},{12,8},{16,12},{20,16},{24,20},{28,24},{32,28},{36,32}... | collective-permute-start | bytes 393224 | tf_op jit(solution)/shard_map/ppermute | solution.py:34
  19.9 1.1 maximum_bitcast_fusion
  21.0 0.9 bitcast_select_fusion
  21.9 3.7 %multiply_add_fusion.1 = f32[16,24,8,256]{3,2,1,0:T(8,128)S(1)} fusion(f32[16,24,8,256]{3,2,1,0:T(8,128)} %param.3, f32[16,24,8,255]{3,2,1,0:T(8,128)} %bitcast.37, f32[24,8,256]{2,1,0:T(8,128)S(1)} %get-tuple-element.25, f32[24,8,256]{2,1,0:T(8,128)S(1)} %get-tuple-element.24), kind=kLoop, calls=%fused_computation.31 | loop fusion | flops 2359296 | bytes 9818112 | tf_op jit(solution)/shard_map/add | solution.py:59
  25.8 0.9 slice.164
  28.2 1.0 fusion.19
  29.3 7.7 %collective-permute-start.4 = (f32[16,1,8,256]{3,2,1,0:T(8,128)S(1)}, f32[16,1,8,256]{3,2,1,0:T(8,128)S(1)}, u32[]{:S(2)}, u32[]{:S(2)}) collective-permute-start(f32[16,1,8,256]{3,2,1,0:T(8,128)S(1)} %get-tuple-element.20), channel_id=1, source_target_pairs={{4,0},{8,4},{12,8},{16,12},{20,16},{24,20},{28,24},{32,28},{36,32}... | collective-permute-start | bytes 393224 | tf_op jit(solution)/shard_map/ppermute | solution.py:34
  37.1 1.0 multiply_add_fusion
  38.1 2.5 %slice.170 = f32[16,24,8,255]{3,2,1,0:T(8,128)} slice(f32[16,24,8,256]{3,2,1,0:T(8,128)S(1)} %multiply_add_fusion), slice={[0:16], [0:24], [0:8], [1:256]} | slice | bytes 6266880 | tf_op jit(solution)/shard_map/slice | solution.py:49
  41.5 2.8 %fusion.17 = f32[16,24,8,256]{3,2,1,0:T(8,128)S(1)} fusion(f32[16,24,8,256]{3,2,1,0:T(8,128)S(1)} %fusion.19, f32[16,25,8,256]{3,2,1,0:T(8,128)S(1)} %fusion.1, f32[16,24,8,256]{3,2,1,0:T(8,128)S(1)} %multiply_add_fusion, f32[16,24,8,255]{3,2,1,0:T(8,128)} %slice.170, f32[24,8,256]{2,1,0:T(8,128)S(1)} %copy-done.8), kind=kLoop, calls=%fused_computation.26 | loop fusion | flops 3932160 | bytes 19058688 | tf_op jit(solution)/shard_map/mul | solution.py:97
  44.5 7.7 %collective-permute-start.6 = (f32[16,1,8,256]{3,2,1,0:T(8,128)S(1)}, f32[16,1,8,256]{3,2,1,0:T(8,128)S(1)}, u32[]{:S(2)}, u32[]{:S(2)}) collective-permute-start(f32[16,1,8,256]{3,2,1,0:T(8,128)S(1)} %get-tuple-element.19), channel_id=1, source_target_pairs={{4,0},{8,4},{12,8},{16,12},{20,16},{24,20},{28,24},{32,28},{36,32}... | collective-permute-start | bytes 393224 | tf_op jit(solution)/shard_map/ppermute | solution.py:34
  52.2 1.1 fusion.31
  53.3 1.8 %collective-permute-done.5 = f32[16,1,8,256]{3,2,1,0:T(8,128)S(1)} collective-permute-done((f32[16,1,8,256]{3,2,1,0:T(8,128)S(1)}, f32[16,1,8,256]{3,2,1,0:T(8,128)S(1)}, u32[]{:S(2)}, u32[]{:S(2)}) %collective-permute-start.5) | collective-permute-done | bytes 131104 | tf_op jit(solution)/shard_map/ppermute | solution.py:31
  55.2 2.2 %fusion.12 = f32[16,24,8,256]{3,2,1,0:T(8,128)S(1)} fusion(f32[16,1,8,256]{3,2,1,0:T(8,128)S(1)} %collective-permute-done.6, f32[16,24,8,256]{3,2,1,0:T(8,128)S(1)} %fusion.17, f32[16,1,8,256]{3,2,1,0:T(8,128)S(1)} %collective-permute-done.5, f32[16,24,8,255]{3,2,1,0:T(8,128)S(1)} %get-tuple-element.17, f32[16,24,8,255]{3,2,1,0:T(8,128)S(1)} %get-tuple-element.16, ...), kind=kLoop, calls=%fused_computation.19 | loop fusion | flops 8650752 | bytes 13803520 | tf_op jit(solution)/shard_map/add | solution.py:75
  57.5 7.8 %collective-permute-start.8 = (f32[16,1,8,256]{3,2,1,0:T(8,128)S(1)}, f32[16,1,8,256]{3,2,1,0:T(8,128)S(1)}, u32[]{:S(2)}, u32[]{:S(2)}) collective-permute-start(f32[16,1,8,256]{3,2,1,0:T(8,128)S(1)} %get-tuple-element.15), channel_id=1, source_target_pairs={{4,0},{8,4},{12,8},{16,12},{20,16},{24,20},{28,24},{32,28},{36,32}... | collective-permute-start | bytes 393224 | tf_op jit(solution)/shard_map/ppermute | solution.py:34
  65.3 1.2 fusion.29
  66.5 1.7 %collective-permute-done.7 = f32[16,1,8,256]{3,2,1,0:T(8,128)S(1)} collective-permute-done((f32[16,1,8,256]{3,2,1,0:T(8,128)S(1)}, f32[16,1,8,256]{3,2,1,0:T(8,128)S(1)}, u32[]{:S(2)}, u32[]{:S(2)}) %collective-permute-start.7) | collective-permute-done | bytes 131104 | tf_op jit(solution)/shard_map/ppermute | solution.py:31
  68.2 2.6 %fusion.6 = f32[16,24,8,256]{3,2,1,0:T(8,128)S(1)} fusion(f32[16,24,8,256]{3,2,1,0:T(8,128)S(1)} %copy-done, f32[16,1,8,256]{3,2,1,0:T(8,128)S(1)} %collective-permute-done.8, f32[16,24,8,256]{3,2,1,0:T(8,128)S(1)} %fusion.12, f32[16,1,8,256]{3,2,1,0:T(8,128)S(1)} %collective-permute-done.7, f32[16,24,8,255]{3,2,1,0:T(8,128)S(1)} %get-tuple-element.13, ...), kind=kLoop, calls=%fused_computation.11 | loop fusion | flops 9437184 | bytes 16949248 | tf_op jit(solution)/shard_map/add | solution.py:100
  70.8 12.0 %copy.29 = f32[16,24,8,256]{0,2,3,1:T(8,128)} copy(f32[16,24,8,256]{3,2,1,0:T(8,128)S(1)} %fusion.6) | data formatting | bytes 6291456 | tf_op jit(solution)/shard_map/add | solution.py:100
  82.9 10.1 %reduce_sum.9 = f32[16,6,8,64]{0,2,3,1:T(8,128)S(1)} reduce(f32[16,6,4,8,64,4]{0,3,5,4,2,1:T(8,128)} %bitcast.36, f32[]{:T(128)} %constant.53.clone.1), dimensions={2,5}, to_apply=%region_0.1 | reduce | flops 737280 | bytes 3342340 | tf_op jit(solution)/shard_map/reduce_sum | solution.py:102
  93.7 8.5 %all_gather.3 = f32[64,3072]{1,0:T(8,128)S(1)} all-gather(f32[16,3072]{1,0:T(8,128)S(1)} %div.18), channel_id=1, replica_groups=mesh['lon'=64,'probe'=4] {'probe'}, dimensions={0}, use_global_device_ids=true | all-gather | bytes 983040 | tf_op jit(solution)/shard_map/all_gather | solution.py:108
  103.1 5.4 %collective-permute-done.9 = f32[64,64]{0,1:T(8,128)S(1)} collective-permute-done((f32[64,64]{0,1:T(8,128)S(1)}, f32[64,64]{0,1:T(8,128)S(1)}, u32[]{:S(2)}, u32[]{:S(2)}) %collective-permute-start.9) | collective-permute-done | bytes 16416 | tf_op jit(solution)/shard_map/ppermute | solution.py:20
  108.5 3.9 %collective-permute-done.10 = f32[64,64]{0,1:T(8,128)S(1)} collective-permute-done((f32[64,64]{0,1:T(8,128)S(1)}, f32[64,64]{0,1:T(8,128)S(1)}, u32[]{:S(2)}, u32[]{:S(2)}) %collective-permute-start.10) | collective-permute-done | bytes 16416 | tf_op jit(solution)/shard_map/ppermute | solution.py:20
  112.4 5.4 %collective-permute-done.11 = f32[64,64]{0,1:T(8,128)S(1)} collective-permute-done((f32[64,64]{0,1:T(8,128)S(1)}, f32[64,64]{0,1:T(8,128)S(1)}, u32[]{:S(2)}, u32[]{:S(2)}) %collective-permute-start.11) | collective-permute-done | bytes 16416 | tf_op jit(solution)/shard_map/ppermute | solution.py:20
  117.8 4.2 %collective-permute-done.12 = f32[64,64]{0,1:T(8,128)S(1)} collective-permute-done((f32[64,64]{0,1:T(8,128)S(1)}, f32[64,64]{0,1:T(8,128)S(1)}, u32[]{:S(2)}, u32[]{:S(2)}) %collective-permute-start.12) | collective-permute-done | bytes 16416 | tf_op jit(solution)/shard_map/ppermute | solution.py:20
  122.0 4.8 %collective-permute-done.13 = f32[64,64]{0,1:T(8,128)S(1)} collective-permute-done((f32[64,64]{0,1:T(8,128)S(1)}, f32[64,64]{0,1:T(8,128)S(1)}, u32[]{:S(2)}, u32[]{:S(2)}) %collective-permute-start.13) | collective-permute-done | bytes 16416 | tf_op jit(solution)/shard_map/ppermute | solution.py:20
  126.8 1.5 collective-permute-start.14
  128.3 6.3 %collective-permute-done.14 = f32[64,64]{0,1:T(8,128)S(1)} collective-permute-done((f32[64,64]{0,1:T(8,128)S(1)}, f32[64,64]{0,1:T(8,128)S(1)}, u32[]{:S(2)}, u32[]{:S(2)}) %collective-permute-start.14) | collective-permute-done | bytes 16416 | tf_op jit(solution)/shard_map/ppermute | solution.py:20
  134.7 5.8 %cholesky.17 = f32[64,64]{1,0:T(8,128)S(1)} custom-call(f32[64,64]{1,0:T(8,128)S(1)} %fusion.24), custom_call_target="Cholesky" | custom-call | tf_op jit(solution)/shard_map/jit(cholesky)/cholesky | solution.py:116
  141.9 4.9 %custom-call.6 = f32[1,64,64]{1,2,0:T(8,128)S(1)} custom-call(f32[1,64,64]{2,1,0:T(8,128)S(1)} %get-tuple-element.34), custom_call_target="InvertDiagBlocksLowerTriangular" | custom-call | tf_op jit(solution)/shard_map/triangular_solve | solution.py:117
  (66 shorter events, 8.7 us)
Async XLA Ops:
  1.3 25.4 %collective-permute-start = (f32[1,8,256]{2,1,0:T(8,128)S(1)}, f32[1,8,256]{2,1,0:T(8,128)S(1)}, u32[]{:S(2)}, u32[]{:S(2)}) collective-permute-start(f32[1,8,256]{2,1,0:T(8,128)S(1)} %slice_bitcast_fusion.1), channel_id=1, source_target_pairs={{4,0},{8,4},{12,8},{16,12},{20,16},{24,20},{28,24},{32,28},{36,32}... | collective-permute-start | bytes 24584 | tf_op jit(solution)/shard_map/ppermute | solution.py:10
  12.1 14.9 %collective-permute-start.1 = (f32[16,1,8,256]{3,2,1,0:T(8,128)S(1)}, f32[16,1,8,256]{3,2,1,0:T(8,128)S(1)}, u32[]{:S(2)}, u32[]{:S(2)}) collective-permute-start(f32[16,1,8,256]{3,2,1,0:T(8,128)S(1)} %get-tuple-element.23), channel_id=1, source_target_pairs={{0,4},{4,8},{8,12},{12,16},{16,20},{20,24},{24,28},{28,32},{32,36}... | collective-permute-start | bytes 393224 | tf_op jit(solution)/shard_map/ppermute | solution.py:31
  12.2 14.8 %collective-permute-start.2 = (f32[16,1,8,256]{3,2,1,0:T(8,128)S(1)}, f32[16,1,8,256]{3,2,1,0:T(8,128)S(1)}, u32[]{:S(2)}, u32[]{:S(2)}) collective-permute-start(f32[16,1,8,256]{3,2,1,0:T(8,128)S(1)} %get-tuple-element.22), channel_id=1, source_target_pairs={{4,0},{8,4},{12,8},{16,12},{20,16},{24,20},{28,24},{32,28},{36,32}... | collective-permute-start | bytes 393224 | tf_op jit(solution)/shard_map/ppermute | solution.py:34
  25.8 1.1 copy-start.7
  25.8 2.0 %copy-start = (f32[16,24,8,256]{3,2,1,0:T(8,128)S(1)}, f32[16,24,8,256]{3,2,1,0:T(8,128)}, u32[]{:S(2)}) copy-start(f32[16,24,8,256]{3,2,1,0:T(8,128)} %param.3) | copy-start | bytes 9437188
  27.0 28.2 %copy-start.1 = (f32[24,8,256]{2,1,0:T(8,128)}, f32[24,8,256]{2,1,0:T(8,128)S(1)}, u32[]{:S(2)}) copy-start(f32[24,8,256]{2,1,0:T(8,128)S(1)} %get-tuple-element.28) | copy-start | bytes 589828
  27.0 28.2 %copy-start.3 = (f32[24,8,256]{2,1,0:T(8,128)}, f32[24,8,256]{2,1,0:T(8,128)S(1)}, u32[]{:S(2)}) copy-start(f32[24,8,256]{2,1,0:T(8,128)S(1)} %get-tuple-element.29) | copy-start | bytes 589828
  27.0 28.2 %copy-start.5 = (f32[24,8,256]{2,1,0:T(8,128)}, f32[24,8,256]{2,1,0:T(8,128)S(1)}, u32[]{:S(2)}) copy-start(f32[24,8,256]{2,1,0:T(8,128)S(1)} %get-tuple-element.32) | copy-start | bytes 589828
  29.3 11.3 %collective-permute-start.3 = (f32[16,1,8,256]{3,2,1,0:T(8,128)S(1)}, f32[16,1,8,256]{3,2,1,0:T(8,128)S(1)}, u32[]{:S(2)}, u32[]{:S(2)}) collective-permute-start(f32[16,1,8,256]{3,2,1,0:T(8,128)S(1)} %get-tuple-element.21), channel_id=1, source_target_pairs={{0,4},{4,8},{8,12},{12,16},{16,20},{20,24},{24,28},{28,32},{32,36}... | collective-permute-start | bytes 393224 | tf_op jit(solution)/shard_map/ppermute | solution.py:31
  29.3 11.2 %collective-permute-start.4 = (f32[16,1,8,256]{3,2,1,0:T(8,128)S(1)}, f32[16,1,8,256]{3,2,1,0:T(8,128)S(1)}, u32[]{:S(2)}, u32[]{:S(2)}) collective-permute-start(f32[16,1,8,256]{3,2,1,0:T(8,128)S(1)} %get-tuple-element.20), channel_id=1, source_target_pairs={{4,0},{8,4},{12,8},{16,12},{20,16},{24,20},{28,24},{32,28},{36,32}... | collective-permute-start | bytes 393224 | tf_op jit(solution)/shard_map/ppermute | solution.py:34
  40.6 0.9 copy-start.8
  44.4 10.8 %collective-permute-start.5 = (f32[16,1,8,256]{3,2,1,0:T(8,128)S(1)}, f32[16,1,8,256]{3,2,1,0:T(8,128)S(1)}, u32[]{:S(2)}, u32[]{:S(2)}) collective-permute-start(f32[16,1,8,256]{3,2,1,0:T(8,128)S(1)} %get-tuple-element.18), channel_id=1, source_target_pairs={{0,4},{4,8},{8,12},{12,16},{16,20},{20,24},{24,28},{28,32},{32,36}... | collective-permute-start | bytes 393224 | tf_op jit(solution)/shard_map/ppermute | solution.py:31
  44.5 10.7 %collective-permute-start.6 = (f32[16,1,8,256]{3,2,1,0:T(8,128)S(1)}, f32[16,1,8,256]{3,2,1,0:T(8,128)S(1)}, u32[]{:S(2)}, u32[]{:S(2)}) collective-permute-start(f32[16,1,8,256]{3,2,1,0:T(8,128)S(1)} %get-tuple-element.19), channel_id=1, source_target_pairs={{4,0},{8,4},{12,8},{16,12},{20,16},{24,20},{28,24},{32,28},{36,32}... | collective-permute-start | bytes 393224 | tf_op jit(solution)/shard_map/ppermute | solution.py:34
  57.4 10.8 %collective-permute-start.7 = (f32[16,1,8,256]{3,2,1,0:T(8,128)S(1)}, f32[16,1,8,256]{3,2,1,0:T(8,128)S(1)}, u32[]{:S(2)}, u32[]{:S(2)}) collective-permute-start(f32[16,1,8,256]{3,2,1,0:T(8,128)S(1)} %get-tuple-element.14), channel_id=1, source_target_pairs={{0,4},{4,8},{8,12},{12,16},{16,20},{20,24},{24,28},{28,32},{32,36}... | collective-permute-start | bytes 393224 | tf_op jit(solution)/shard_map/ppermute | solution.py:31
  57.5 10.7 %copy-start.2 = (f32[24,8,256]{2,1,0:T(8,128)S(1)}, f32[24,8,256]{2,1,0:T(8,128)}, u32[]{:S(2)}) copy-start(f32[24,8,256]{2,1,0:T(8,128)} %copy-done.1) | copy-start | bytes 589828
  57.5 10.7 %copy-start.4 = (f32[24,8,256]{2,1,0:T(8,128)S(1)}, f32[24,8,256]{2,1,0:T(8,128)}, u32[]{:S(2)}) copy-start(f32[24,8,256]{2,1,0:T(8,128)} %copy-done.3) | copy-start | bytes 589828
  57.5 10.7 %copy-start.6 = (f32[24,8,256]{2,1,0:T(8,128)S(1)}, f32[24,8,256]{2,1,0:T(8,128)}, u32[]{:S(2)}) copy-start(f32[24,8,256]{2,1,0:T(8,128)} %copy-done.5) | copy-start | bytes 589828
  57.5 10.6 %collective-permute-start.8 = (f32[16,1,8,256]{3,2,1,0:T(8,128)S(1)}, f32[16,1,8,256]{3,2,1,0:T(8,128)S(1)}, u32[]{:S(2)}, u32[]{:S(2)}) collective-permute-start(f32[16,1,8,256]{3,2,1,0:T(8,128)S(1)} %get-tuple-element.15), channel_id=1, source_target_pairs={{4,0},{8,4},{12,8},{16,12},{20,16},{24,20},{28,24},{32,28},{36,32}... | collective-permute-start | bytes 393224 | tf_op jit(solution)/shard_map/ppermute | solution.py:34
  103.0 5.5 %collective-permute-start.9 = (f32[64,64]{0,1:T(8,128)S(1)}, f32[64,64]{0,1:T(8,128)S(1)}, u32[]{:S(2)}, u32[]{:S(2)}) collective-permute-start(f32[64,64]{0,1:T(8,128)S(1)} %fusion.35), channel_id=1, source_target_pairs={{0,4},{4,0},{8,12},{12,8},{16,20},{20,16},{24,28},{28,24},{32,36},... | collective-permute-start | bytes 49160 | tf_op jit(solution)/shard_map/ppermute | solution.py:20
  108.5 3.9 %collective-permute-start.10 = (f32[64,64]{0,1:T(8,128)S(1)}, f32[64,64]{0,1:T(8,128)S(1)}, u32[]{:S(2)}, u32[]{:S(2)}) collective-permute-start(f32[64,64]{0,1:T(8,128)S(1)} %add.96), channel_id=1, source_target_pairs={{0,8},{4,12},{8,0},{12,4},{16,24},{20,28},{24,16},{28,20},{32,40},... | collective-permute-start | bytes 49160 | tf_op jit(solution)/shard_map/ppermute | solution.py:20
  112.4 5.4 %collective-permute-start.11 = (f32[64,64]{0,1:T(8,128)S(1)}, f32[64,64]{0,1:T(8,128)S(1)}, u32[]{:S(2)}, u32[]{:S(2)}) collective-permute-start(f32[64,64]{0,1:T(8,128)S(1)} %add.97), channel_id=1, source_target_pairs={{0,16},{4,20},{8,24},{12,28},{16,0},{20,4},{24,8},{28,12},{32,48},... | collective-permute-start | bytes 49160 | tf_op jit(solution)/shard_map/ppermute | solution.py:20
  117.8 4.2 %collective-permute-start.12 = (f32[64,64]{0,1:T(8,128)S(1)}, f32[64,64]{0,1:T(8,128)S(1)}, u32[]{:S(2)}, u32[]{:S(2)}) collective-permute-start(f32[64,64]{0,1:T(8,128)S(1)} %add.98), channel_id=1, source_target_pairs={{0,32},{4,36},{8,40},{12,44},{16,48},{20,52},{24,56},{28,60},{32,0... | collective-permute-start | bytes 49160 | tf_op jit(solution)/shard_map/ppermute | solution.py:20
  122.0 4.8 %collective-permute-start.13 = (f32[64,64]{0,1:T(8,128)S(1)}, f32[64,64]{0,1:T(8,128)S(1)}, u32[]{:S(2)}, u32[]{:S(2)}) collective-permute-start(f32[64,64]{0,1:T(8,128)S(1)} %add.99), channel_id=1, source_target_pairs={{0,64},{4,68},{8,72},{12,76},{16,80},{20,84},{24,88},{28,92},{32,9... | collective-permute-start | bytes 49160 | tf_op jit(solution)/shard_map/ppermute | solution.py:20
  126.8 7.8 %collective-permute-start.14 = (f32[64,64]{0,1:T(8,128)S(1)}, f32[64,64]{0,1:T(8,128)S(1)}, u32[]{:S(2)}, u32[]{:S(2)}) collective-permute-start(f32[64,64]{0,1:T(8,128)S(1)} %add.100), channel_id=1, source_target_pairs={{0,128},{4,132},{8,136},{12,140},{16,144},{20,148},{24,152},{28,15... | collective-permute-start | bytes 49160 | tf_op jit(solution)/shard_map/ppermute | solution.py:20
where the time goes:
time: 149 us
  starting transfers between devices  42.7 us (29%)
  other arithmetic  38.7 us (26%)
  waiting for transfers between devices  33.5 us (22%)
  local copies, waits for them, and re-layouts  23 us (15%)
  blocking collectives  8.45 us (6%)
    ppermute x4, starting transfers between devices, padded(): lax.ppermute(lax.slice_in_dim(block, 0, width, axis=dim), axis, backward)  31 us
    ppermute x6, waiting for transfers between devices, butterfly_sum(): block = block + lax.ppermute(block, axis, route)  30 us
    add x1, local copies, waits for them, and re-layouts, body(): sketch = increments + state  12 us
    reduce_sum x1, other arithmetic, body(): jnp.mean(sketch.reshape(probe_count, lon_count // 4, 4, level_count, lat_...  10.1 us
    ppermute x1, starting transfers between devices, from_behind(): return lax.ppermute(block, axis, route)  9.78 us
    all_gather x1, blocking collectives, body(): full_panel = lax.all_gather(coarse, 'probe', axis=0, tiled=True)  8.45 us
    another operation x3, other arithmetic, body(): lower = jnp.linalg.cholesky(gram)  6.52 us
    another operation x1, other arithmetic, body(): lax.linalg.triangular_solve(lower, ident, left_side=True, lower=True)  4.9 us
  transfers between devices with their start and end apart: 15, of which 8 were waited for; matrix products, arithmetic and copies ran while one was open for 9% of the time, Pallas kernels for 0%

commit v1 on v0

--- a/solution.py
+++ b/solution.py
@@ -105,7 +105,9 @@
     coarse = coarse.reshape(probe_count, -1)
     all_probes = probe_count * lax.axis_size("probe")
     ident = jnp.eye(all_probes, dtype=jnp.float32)
-    full_panel = lax.all_gather(coarse, "probe", axis=0, tiled=True)
+    full_panel = jnp.concatenate(
+        lax.all_to_all(jnp.stack([coarse] * lax.axis_size("probe")), "probe", 0, 0), axis=0
+    )
     local_gram = jnp.dot(
         full_panel,
         full_panel.T,

time: 149 us -> 155 us (1.040)
  blocking collectives: 8.45 us -> 13.7 us
    all_to_all x0 -> x1, blocking collectives: none -> 13.7 us  [body(): lax.all_to_all(jnp.stack([coarse] * lax.axis_size('probe')), 'probe', 0, 0)]
    all_gather x1 -> x0, blocking collectives: 8.45 us -> none  [body(): full_panel = lax.all_gather(coarse, 'probe', axis=0, tiled=True)]
where the time goes in v1:
time: 155 us; the launch traced here: 154 us
  starting transfers between devices  43 us (28%)
  other arithmetic  38.7 us (25%)
  waiting for transfers between devices  33.3 us (21%)
  local copies, waits for them, and re-layouts  22.3 us (14%)
  blocking collectives  13.7 us (9%)
  matrix products  2.17 us (1%)
    ppermute x4, starting transfers between devices, padded(): lax.ppermute(lax.slice_in_dim(block, 0, width, axis=dim), axis, backward)  31 us
    ppermute x6, waiting for transfers between devices, butterfly_sum(): block = block + lax.ppermute(block, axis, route)  29.8 us
    all_to_all x1, blocking collectives, body(): lax.all_to_all(jnp.stack([coarse] * lax.axis_size('probe')), 'probe', 0, 0)  13.7 us
    add x1, local copies, waits for them, and re-layouts, body(): sketch = increments + state  12 us
    reduce_sum x1, other arithmetic, body(): jnp.mean(sketch.reshape(probe_count, lon_count // 4, 4, level_count, lat_...  10.1 us
    ppermute x1, starting transfers between devices, from_behind(): return lax.ppermute(block, axis, route)  9.78 us
    another operation x3, other arithmetic, body(): lower = jnp.linalg.cholesky(gram)  6.52 us
    another operation x1, other arithmetic, body(): lax.linalg.triangular_solve(lower, ident, left_side=True, lower=True)  4.9 us
  transfers between devices with their start and end apart: 15, of which 8 were waited for; matrix products, arithmetic and copies ran while one was open for 9% of the time, Pallas kernels for 0%

profile of v1, /device:TPU:8, one launch (start us, length us, event | category | flops | bytes accessed | tf_op | source)
XLA Modules:
  0.0 154.4 jit_solution(18442409916778070136)
XLA Ops:
  1.3 9.8 %collective-permute-start = (f32[1,8,256]{2,1,0:T(8,128)S(1)}, f32[1,8,256]{2,1,0:T(8,128)S(1)}, u32[]{:S(2)}, u32[]{:S(2)}) collective-permute-start(f32[1,8,256]{2,1,0:T(8,128)S(1)} %slice_bitcast_fusion.1), channel_id=1, source_target_pairs={{4,0},{8,4},{12,8},{16,12},{20,16},{24,20},{28,24},{32,28},{36,32}... | collective-permute-start | bytes 24584 | tf_op jit(solution)/shard_map/ppermute | solution.py:10
  11.1 1.0 fusion.37
  12.2 7.7 %collective-permute-start.2 = (f32[16,1,8,256]{3,2,1,0:T(8,128)S(1)}, f32[16,1,8,256]{3,2,1,0:T(8,128)S(1)}, u32[]{:S(2)}, u32[]{:S(2)}) collective-permute-start(f32[16,1,8,256]{3,2,1,0:T(8,128)S(1)} %get-tuple-element.22), channel_id=1, source_target_pairs={{4,0},{8,4},{12,8},{16,12},{20,16},{24,20},{28,24},{32,28},{36,32}... | collective-permute-start | bytes 393224 | tf_op jit(solution)/shard_map/ppermute | solution.py:34
  19.9 1.1 maximum_bitcast_fusion
  21.0 0.9 bitcast_select_fusion
  21.9 3.7 %multiply_add_fusion.1 = f32[16,24,8,256]{3,2,1,0:T(8,128)S(1)} fusion(f32[16,24,8,256]{3,2,1,0:T(8,128)} %param.3, f32[16,24,8,255]{3,2,1,0:T(8,128)} %bitcast.42, f32[24,8,256]{2,1,0:T(8,128)S(1)} %get-tuple-element.25, f32[24,8,256]{2,1,0:T(8,128)S(1)} %get-tuple-element.24), kind=kLoop, calls=%fused_computation.31 | loop fusion | flops 2359296 | bytes 9818112 | tf_op jit(solution)/shard_map/add | solution.py:59
  28.2 1.0 fusion.19
  29.3 7.7 %collective-permute-start.4 = (f32[16,1,8,256]{3,2,1,0:T(8,128)S(1)}, f32[16,1,8,256]{3,2,1,0:T(8,128)S(1)}, u32[]{:S(2)}, u32[]{:S(2)}) collective-permute-start(f32[16,1,8,256]{3,2,1,0:T(8,128)S(1)} %get-tuple-element.20), channel_id=1, source_target_pairs={{4,0},{8,4},{12,8},{16,12},{20,16},{24,20},{28,24},{32,28},{36,32}... | collective-permute-start | bytes 393224 | tf_op jit(solution)/shard_map/ppermute | solution.py:34
  37.1 1.0 multiply_add_fusion
  38.1 2.5 %slice.170 = f32[16,24,8,255]{3,2,1,0:T(8,128)} slice(f32[16,24,8,256]{3,2,1,0:T(8,128)S(1)} %multiply_add_fusion), slice={[0:16], [0:24], [0:8], [1:256]} | slice | bytes 6266880 | tf_op jit(solution)/shard_map/slice | solution.py:49
  41.5 2.8 %fusion.17 = f32[16,24,8,256]{3,2,1,0:T(8,128)S(1)} fusion(f32[16,24,8,256]{3,2,1,0:T(8,128)S(1)} %fusion.19, f32[16,25,8,256]{3,2,1,0:T(8,128)S(1)} %fusion.1, f32[16,24,8,256]{3,2,1,0:T(8,128)S(1)} %multiply_add_fusion, f32[16,24,8,255]{3,2,1,0:T(8,128)} %slice.170, f32[24,8,256]{2,1,0:T(8,128)S(1)} %copy-done.8), kind=kLoop, calls=%fused_computation.26 | loop fusion | flops 3932160 | bytes 19058688 | tf_op jit(solution)/shard_map/mul | solution.py:97
  44.5 7.7 %collective-permute-start.6 = (f32[16,1,8,256]{3,2,1,0:T(8,128)S(1)}, f32[16,1,8,256]{3,2,1,0:T(8,128)S(1)}, u32[]{:S(2)}, u32[]{:S(2)}) collective-permute-start(f32[16,1,8,256]{3,2,1,0:T(8,128)S(1)} %get-tuple-element.19), channel_id=1, source_target_pairs={{4,0},{8,4},{12,8},{16,12},{20,16},{24,20},{28,24},{32,28},{36,32}... | collective-permute-start | bytes 393224 | tf_op jit(solution)/shard_map/ppermute | solution.py:34
  52.2 1.1 fusion.34
  53.3 1.8 %collective-permute-done.5 = f32[16,1,8,256]{3,2,1,0:T(8,128)S(1)} collective-permute-done((f32[16,1,8,256]{3,2,1,0:T(8,128)S(1)}, f32[16,1,8,256]{3,2,1,0:T(8,128)S(1)}, u32[]{:S(2)}, u32[]{:S(2)}) %collective-permute-start.5) | collective-permute-done | bytes 131104 | tf_op jit(solution)/shard_map/ppermute | solution.py:31
  55.2 2.2 %fusion.12 = f32[16,24,8,256]{3,2,1,0:T(8,128)S(1)} fusion(f32[16,1,8,256]{3,2,1,0:T(8,128)S(1)} %collective-permute-done.6, f32[16,24,8,256]{3,2,1,0:T(8,128)S(1)} %fusion.17, f32[16,1,8,256]{3,2,1,0:T(8,128)S(1)} %collective-permute-done.5, f32[16,24,8,255]{3,2,1,0:T(8,128)S(1)} %get-tuple-element.17, f32[16,24,8,255]{3,2,1,0:T(8,128)S(1)} %get-tuple-element.16, ...), kind=kLoop, calls=%fused_computation.19 | loop fusion | flops 8650752 | bytes 13803520 | tf_op jit(solution)/shard_map/add | solution.py:75
  57.5 7.8 %collective-permute-start.8 = (f32[16,1,8,256]{3,2,1,0:T(8,128)S(1)}, f32[16,1,8,256]{3,2,1,0:T(8,128)S(1)}, u32[]{:S(2)}, u32[]{:S(2)}) collective-permute-start(f32[16,1,8,256]{3,2,1,0:T(8,128)S(1)} %get-tuple-element.15), channel_id=1, source_target_pairs={{4,0},{8,4},{12,8},{16,12},{20,16},{24,20},{28,24},{32,28},{36,32}... | collective-permute-start | bytes 393224 | tf_op jit(solution)/shard_map/ppermute | solution.py:34
  65.3 1.2 fusion.32
  66.5 1.7 %collective-permute-done.7 = f32[16,1,8,256]{3,2,1,0:T(8,128)S(1)} collective-permute-done((f32[16,1,8,256]{3,2,1,0:T(8,128)S(1)}, f32[16,1,8,256]{3,2,1,0:T(8,128)S(1)}, u32[]{:S(2)}, u32[]{:S(2)}) %collective-permute-start.7) | collective-permute-done | bytes 131104 | tf_op jit(solution)/shard_map/ppermute | solution.py:31
  68.2 2.6 %fusion.6 = f32[16,24,8,256]{3,2,1,0:T(8,128)S(1)} fusion(f32[16,24,8,256]{3,2,1,0:T(8,128)S(1)} %copy-done, f32[16,1,8,256]{3,2,1,0:T(8,128)S(1)} %collective-permute-done.8, f32[16,24,8,256]{3,2,1,0:T(8,128)S(1)} %fusion.12, f32[16,1,8,256]{3,2,1,0:T(8,128)S(1)} %collective-permute-done.7, f32[16,24,8,255]{3,2,1,0:T(8,128)S(1)} %get-tuple-element.13, ...), kind=kLoop, calls=%fused_computation.11 | loop fusion | flops 9437184 | bytes 16949248 | tf_op jit(solution)/shard_map/add | solution.py:100
  70.8 12.0 %copy.28 = f32[16,24,8,256]{0,2,3,1:T(8,128)} copy(f32[16,24,8,256]{3,2,1,0:T(8,128)S(1)} %fusion.6) | data formatting | bytes 6291456 | tf_op jit(solution)/shard_map/add | solution.py:100
  82.9 10.1 %reduce_sum.9 = f32[16,6,8,64]{0,2,3,1:T(8,128)S(1)} reduce(f32[16,6,4,8,64,4]{0,3,5,4,2,1:T(8,128)} %bitcast.41, f32[]{:T(128)} %constant.53.clone.1), dimensions={2,5}, to_apply=%region_0.1 | reduce | flops 737280 | bytes 3342340 | tf_op jit(solution)/shard_map/reduce_sum | solution.py:102
  93.8 13.7 %all_to_all.5 = f32[4,16,3072]{2,1,0:T(8,128)S(1)} all-to-all(f32[4,16,3072]{2,1,0:T(8,128)S(1)} %stack.3), channel_id=1, replica_groups=mesh['lon'=64,'probe'=4] {'probe'}, dimensions={0} | all-to-all | bytes 1572864 | tf_op jit(solution)/shard_map/all_to_all | solution.py:109
  108.4 5.4 %collective-permute-done.9 = f32[64,64]{0,1:T(8,128)S(1)} collective-permute-done((f32[64,64]{0,1:T(8,128)S(1)}, f32[64,64]{0,1:T(8,128)S(1)}, u32[]{:S(2)}, u32[]{:S(2)}) %collective-permute-start.9) | collective-permute-done | bytes 16416 | tf_op jit(solution)/shard_map/ppermute | solution.py:20
  113.8 3.9 %collective-permute-done.10 = f32[64,64]{0,1:T(8,128)S(1)} collective-permute-done((f32[64,64]{0,1:T(8,128)S(1)}, f32[64,64]{0,1:T(8,128)S(1)}, u32[]{:S(2)}, u32[]{:S(2)}) %collective-permute-start.10) | collective-permute-done | bytes 16416 | tf_op jit(solution)/shard_map/ppermute | solution.py:20
  117.8 5.4 %collective-permute-done.11 = f32[64,64]{0,1:T(8,128)S(1)} collective-permute-done((f32[64,64]{0,1:T(8,128)S(1)}, f32[64,64]{0,1:T(8,128)S(1)}, u32[]{:S(2)}, u32[]{:S(2)}) %collective-permute-start.11) | collective-permute-done | bytes 16416 | tf_op jit(solution)/shard_map/ppermute | solution.py:20
  123.2 3.9 %collective-permute-done.12 = f32[64,64]{0,1:T(8,128)S(1)} collective-permute-done((f32[64,64]{0,1:T(8,128)S(1)}, f32[64,64]{0,1:T(8,128)S(1)}, u32[]{:S(2)}, u32[]{:S(2)}) %collective-permute-start.12) | collective-permute-done | bytes 16416 | tf_op jit(solution)/shard_map/ppermute | solution.py:20
  127.1 5.2 %collective-permute-done.13 = f32[64,64]{0,1:T(8,128)S(1)} collective-permute-done((f32[64,64]{0,1:T(8,128)S(1)}, f32[64,64]{0,1:T(8,128)S(1)}, u32[]{:S(2)}, u32[]{:S(2)}) %collective-permute-start.13) | collective-permute-done | bytes 16416 | tf_op jit(solution)/shard_map/ppermute | solution.py:20
  132.3 1.8 %collective-permute-start.14 = (f32[64,64]{0,1:T(8,128)S(1)}, f32[64,64]{0,1:T(8,128)S(1)}, u32[]{:S(2)}, u32[]{:S(2)}) collective-permute-start(f32[64,64]{0,1:T(8,128)S(1)} %add.100), channel_id=1, source_target_pairs={{0,128},{4,132},{8,136},{12,140},{16,144},{20,148},{24,152},{28,15... | collective-permute-start | bytes 49160 | tf_op jit(solution)/shard_map/ppermute | solution.py:20
  134.1 6.0 %collective-permute-done.14 = f32[64,64]{0,1:T(8,128)S(1)} collective-permute-done((f32[64,64]{0,1:T(8,128)S(1)}, f32[64,64]{0,1:T(8,128)S(1)}, u32[]{:S(2)}, u32[]{:S(2)}) %collective-permute-start.14) | collective-permute-done | bytes 16416 | tf_op jit(solution)/shard_map/ppermute | solution.py:20
  140.2 5.8 %cholesky.17 = f32[64,64]{1,0:T(8,128)S(1)} custom-call(f32[64,64]{1,0:T(8,128)S(1)} %fusion.27), custom_call_target="Cholesky" | custom-call | tf_op jit(solution)/shard_map/jit(cholesky)/cholesky | solution.py:118
  147.4 4.9 %custom-call.6 = f32[1,64,64]{1,2,0:T(8,128)S(1)} custom-call(f32[1,64,64]{2,1,0:T(8,128)S(1)} %get-tuple-element.34), custom_call_target="InvertDiagBlocksLowerTriangular" | custom-call | tf_op jit(solution)/shard_map/triangular_solve | solution.py:119
  153.2 1.2 fusion.20
  (66 shorter events, 8.5 us)
Async XLA Ops:
  1.3 25.4 %collective-permute-start = (f32[1,8,256]{2,1,0:T(8,128)S(1)}, f32[1,8,256]{2,1,0:T(8,128)S(1)}, u32[]{:S(2)}, u32[]{:S(2)}) collective-permute-start(f32[1,8,256]{2,1,0:T(8,128)S(1)} %slice_bitcast_fusion.1), channel_id=1, source_target_pairs={{4,0},{8,4},{12,8},{16,12},{20,16},{24,20},{28,24},{32,28},{36,32}... | collective-permute-start | bytes 24584 | tf_op jit(solution)/shard_map/ppermute | solution.py:10
  12.1 14.9 %collective-permute-start.1 = (f32[16,1,8,256]{3,2,1,0:T(8,128)S(1)}, f32[16,1,8,256]{3,2,1,0:T(8,128)S(1)}, u32[]{:S(2)}, u32[]{:S(2)}) collective-permute-start(f32[16,1,8,256]{3,2,1,0:T(8,128)S(1)} %get-tuple-element.23), channel_id=1, source_target_pairs={{0,4},{4,8},{8,12},{12,16},{16,20},{20,24},{24,28},{28,32},{32,36}... | collective-permute-start | bytes 393224 | tf_op jit(solution)/shard_map/ppermute | solution.py:31
  12.2 14.8 %collective-permute-start.2 = (f32[16,1,8,256]{3,2,1,0:T(8,128)S(1)}, f32[16,1,8,256]{3,2,1,0:T(8,128)S(1)}, u32[]{:S(2)}, u32[]{:S(2)}) collective-permute-start(f32[16,1,8,256]{3,2,1,0:T(8,128)S(1)} %get-tuple-element.22), channel_id=1, source_target_pairs={{4,0},{8,4},{12,8},{16,12},{20,16},{24,20},{28,24},{32,28},{36,32}... | collective-permute-start | bytes 393224 | tf_op jit(solution)/shard_map/ppermute | solution.py:34
  25.8 1.1 copy-start.7
  25.8 2.0 %copy-start = (f32[16,24,8,256]{3,2,1,0:T(8,128)S(1)}, f32[16,24,8,256]{3,2,1,0:T(8,128)}, u32[]{:S(2)}) copy-start(f32[16,24,8,256]{3,2,1,0:T(8,128)} %param.3) | copy-start | bytes 9437188
  27.0 28.2 %copy-start.1 = (f32[24,8,256]{2,1,0:T(8,128)}, f32[24,8,256]{2,1,0:T(8,128)S(1)}, u32[]{:S(2)}) copy-start(f32[24,8,256]{2,1,0:T(8,128)S(1)} %get-tuple-element.28) | copy-start | bytes 589828
  27.0 28.2 %copy-start.3 = (f32[24,8,256]{2,1,0:T(8,128)}, f32[24,8,256]{2,1,0:T(8,128)S(1)}, u32[]{:S(2)}) copy-start(f32[24,8,256]{2,1,0:T(8,128)S(1)} %get-tuple-element.29) | copy-start | bytes 589828
  27.0 28.2 %copy-start.5 = (f32[24,8,256]{2,1,0:T(8,128)}, f32[24,8,256]{2,1,0:T(8,128)S(1)}, u32[]{:S(2)}) copy-start(f32[24,8,256]{2,1,0:T(8,128)S(1)} %get-tuple-element.32) | copy-start | bytes 589828
  29.3 11.3 %collective-permute-start.3 = (f32[16,1,8,256]{3,2,1,0:T(8,128)S(1)}, f32[16,1,8,256]{3,2,1,0:T(8,128)S(1)}, u32[]{:S(2)}, u32[]{:S(2)}) collective-permute-start(f32[16,1,8,256]{3,2,1,0:T(8,128)S(1)} %get-tuple-element.21), channel_id=1, source_target_pairs={{0,4},{4,8},{8,12},{12,16},{16,20},{20,24},{24,28},{28,32},{32,36}... | collective-permute-start | bytes 393224 | tf_op jit(solution)/shard_map/ppermute | solution.py:31
  29.3 11.2 %collective-permute-start.4 = (f32[16,1,8,256]{3,2,1,0:T(8,128)S(1)}, f32[16,1,8,256]{3,2,1,0:T(8,128)S(1)}, u32[]{:S(2)}, u32[]{:S(2)}) collective-permute-start(f32[16,1,8,256]{3,2,1,0:T(8,128)S(1)} %get-tuple-element.20), channel_id=1, source_target_pairs={{4,0},{8,4},{12,8},{16,12},{20,16},{24,20},{28,24},{32,28},{36,32}... | collective-permute-start | bytes 393224 | tf_op jit(solution)/shard_map/ppermute | solution.py:34
  40.6 0.9 copy-start.8
  44.4 10.8 %collective-permute-start.5 = (f32[16,1,8,256]{3,2,1,0:T(8,128)S(1)}, f32[16,1,8,256]{3,2,1,0:T(8,128)S(1)}, u32[]{:S(2)}, u32[]{:S(2)}) collective-permute-start(f32[16,1,8,256]{3,2,1,0:T(8,128)S(1)} %get-tuple-element.18), channel_id=1, source_target_pairs={{0,4},{4,8},{8,12},{12,16},{16,20},{20,24},{24,28},{28,32},{32,36}... | collective-permute-start | bytes 393224 | tf_op jit(solution)/shard_map/ppermute | solution.py:31
  44.5 10.7 %collective-permute-start.6 = (f32[16,1,8,256]{3,2,1,0:T(8,128)S(1)}, f32[16,1,8,256]{3,2,1,0:T(8,128)S(1)}, u32[]{:S(2)}, u32[]{:S(2)}) collective-permute-start(f32[16,1,8,256]{3,2,1,0:T(8,128)S(1)} %get-tuple-element.19), channel_id=1, source_target_pairs={{4,0},{8,4},{12,8},{16,12},{20,16},{24,20},{28,24},{32,28},{36,32}... | collective-permute-start | bytes 393224 | tf_op jit(solution)/shard_map/ppermute | solution.py:34
  57.4 10.8 %collective-permute-start.7 = (f32[16,1,8,256]{3,2,1,0:T(8,128)S(1)}, f32[16,1,8,256]{3,2,1,0:T(8,128)S(1)}, u32[]{:S(2)}, u32[]{:S(2)}) collective-permute-start(f32[16,1,8,256]{3,2,1,0:T(8,128)S(1)} %get-tuple-element.14), channel_id=1, source_target_pairs={{0,4},{4,8},{8,12},{12,16},{16,20},{20,24},{24,28},{28,32},{32,36}... | collective-permute-start | bytes 393224 | tf_op jit(solution)/shard_map/ppermute | solution.py:31
  57.5 10.7 %copy-start.2 = (f32[24,8,256]{2,1,0:T(8,128)S(1)}, f32[24,8,256]{2,1,0:T(8,128)}, u32[]{:S(2)}) copy-start(f32[24,8,256]{2,1,0:T(8,128)} %copy-done.1) | copy-start | bytes 589828
  57.5 10.7 %copy-start.4 = (f32[24,8,256]{2,1,0:T(8,128)S(1)}, f32[24,8,256]{2,1,0:T(8,128)}, u32[]{:S(2)}) copy-start(f32[24,8,256]{2,1,0:T(8,128)} %copy-done.3) | copy-start | bytes 589828
  57.5 10.7 %copy-start.6 = (f32[24,8,256]{2,1,0:T(8,128)S(1)}, f32[24,8,256]{2,1,0:T(8,128)}, u32[]{:S(2)}) copy-start(f32[24,8,256]{2,1,0:T(8,128)} %copy-done.5) | copy-start | bytes 589828
  57.5 10.6 %collective-permute-start.8 = (f32[16,1,8,256]{3,2,1,0:T(8,128)S(1)}, f32[16,1,8,256]{3,2,1,0:T(8,128)S(1)}, u32[]{:S(2)}, u32[]{:S(2)}) collective-permute-start(f32[16,1,8,256]{3,2,1,0:T(8,128)S(1)} %get-tuple-element.15), channel_id=1, source_target_pairs={{4,0},{8,4},{12,8},{16,12},{20,16},{24,20},{28,24},{32,28},{36,32}... | collective-permute-start | bytes 393224 | tf_op jit(solution)/shard_map/ppermute | solution.py:34
  108.3 5.5 %collective-permute-start.9 = (f32[64,64]{0,1:T(8,128)S(1)}, f32[64,64]{0,1:T(8,128)S(1)}, u32[]{:S(2)}, u32[]{:S(2)}) collective-permute-start(f32[64,64]{0,1:T(8,128)S(1)} %fusion.38), channel_id=1, source_target_pairs={{0,4},{4,0},{8,12},{12,8},{16,20},{20,16},{24,28},{28,24},{32,36},... | collective-permute-start | bytes 49160 | tf_op jit(solution)/shard_map/ppermute | solution.py:20
  113.8 3.9 %collective-permute-start.10 = (f32[64,64]{0,1:T(8,128)S(1)}, f32[64,64]{0,1:T(8,128)S(1)}, u32[]{:S(2)}, u32[]{:S(2)}) collective-permute-start(f32[64,64]{0,1:T(8,128)S(1)} %add.96), channel_id=1, source_target_pairs={{0,8},{4,12},{8,0},{12,4},{16,24},{20,28},{24,16},{28,20},{32,40},... | collective-permute-start | bytes 49160 | tf_op jit(solution)/shard_map/ppermute | solution.py:20
  117.8 5.4 %collective-permute-start.11 = (f32[64,64]{0,1:T(8,128)S(1)}, f32[64,64]{0,1:T(8,128)S(1)}, u32[]{:S(2)}, u32[]{:S(2)}) collective-permute-start(f32[64,64]{0,1:T(8,128)S(1)} %add.97), channel_id=1, source_target_pairs={{0,16},{4,20},{8,24},{12,28},{16,0},{20,4},{24,8},{28,12},{32,48},... | collective-permute-start | bytes 49160 | tf_op jit(solution)/shard_map/ppermute | solution.py:20
  123.2 3.9 %collective-permute-start.12 = (f32[64,64]{0,1:T(8,128)S(1)}, f32[64,64]{0,1:T(8,128)S(1)}, u32[]{:S(2)}, u32[]{:S(2)}) collective-permute-start(f32[64,64]{0,1:T(8,128)S(1)} %add.98), channel_id=1, source_target_pairs={{0,32},{4,36},{8,40},{12,44},{16,48},{20,52},{24,56},{28,60},{32,0... | collective-permute-start | bytes 49160 | tf_op jit(solution)/shard_map/ppermute | solution.py:20
  127.1 5.2 %collective-permute-start.13 = (f32[64,64]{0,1:T(8,128)S(1)}, f32[64,64]{0,1:T(8,128)S(1)}, u32[]{:S(2)}, u32[]{:S(2)}) collective-permute-start(f32[64,64]{0,1:T(8,128)S(1)} %add.99), channel_id=1, source_target_pairs={{0,64},{4,68},{8,72},{12,76},{16,80},{20,84},{24,88},{28,92},{32,9... | collective-permute-start | bytes 49160 | tf_op jit(solution)/shard_map/ppermute | solution.py:20
  132.3 7.8 %collective-permute-start.14 = (f32[64,64]{0,1:T(8,128)S(1)}, f32[64,64]{0,1:T(8,128)S(1)}, u32[]{:S(2)}, u32[]{:S(2)}) collective-permute-start(f32[64,64]{0,1:T(8,128)S(1)} %add.100), channel_id=1, source_target_pairs={{0,128},{4,132},{8,136},{12,140},{16,144},{20,148},{24,152},{28,15... | collective-permute-start | bytes 49160 | tf_op jit(solution)/shard_map/ppermute | solution.py:20
